TPU v7x, 32 devices: a whole 2x2x4 slice. The times are simulated.
32 devices in a mesh: seq: 8 (over y, x, core), ch: 4 (over z).
Axes of the slice: x: 2, y: 2, z: 4, core: 2. Of those that a mesh axis runs over, the one named last changes fastest.
Arguments:
- out_gate: bfloat16 [4096, 1024], P('ch', 'seq'), may hold values from -6 to 6
- key_proj: bfloat16 [4096, 1024], P('ch', 'seq'), may hold values from -6 to 6
- value_proj: bfloat16 [4096, 1024], P('ch', 'seq'), may hold values from -6 to 6
- long_filter: bfloat16 [4096, 1024], P('ch', 'seq'), may hold values from -0.1875 to 0.1875
- skip_gain: float32 [4096], P('ch'), may hold values from -4 to 4
- residual: bfloat16 [4096, 1024], P('ch', 'seq'), may hold values from -6 to 6
- norm_gain: float32 [4096], P('ch'), may hold values from 0.5 to 1.5
Outputs:
- mixed: bfloat16 [4096, 1024], P('ch', 'seq')
- normed: bfloat16 [4096, 1024], P('ch', 'seq')
All inputs are finite; a program needn't handle non-finite values.
Results may differ from a plain program's by a relative error of at most 0.0075.
Values may be sent and summed in bfloat16 or wider, within the bound.
A program may use at most 64 MiB of HBM per device.

v0:
```python
import math
import jax
import jax.numpy as jnp
from jax import lax
from jax.sharding import PartitionSpec as P

D = 4096
HIGHEST = lax.Precision.HIGHEST


def tables(count, span, period):
    row_ids = jnp.arange(count, dtype=jnp.int32)[:, None]
    col_ids = jnp.arange(span, dtype=jnp.int32)[None, :]
    phases = (row_ids * col_ids % period).astype(jnp.float32) * (2.0 * math.pi / period)
    return (jnp.cos(phases), jnp.sin(phases))


def product(left, right):
    return jnp.dot(left, right, precision=HIGHEST, preferred_element_type=jnp.float32)


def block_spectrum(signal):
    width = signal.shape[1]
    cosine, sine = tables(width, 2 * width, 2 * width)
    return (product(signal, cosine), -product(signal, sine))


def block_inverse(real_part, imag_part):
    span = real_part.shape[1]
    cosine, sine = tables(span, span, span)
    return (product(real_part, cosine) - product(imag_part, sine)) / span


def index_convolve(input_real, input_imag, filter_real, filter_imag):
    blocks = input_real.shape[0]
    forward_cos, forward_sin = tables(2 * blocks, blocks, 2 * blocks)

    def forward(real_part, imag_part):
        return (
            product(forward_cos, real_part) + product(forward_sin, imag_part),
            product(forward_cos, imag_part) - product(forward_sin, real_part),
        )

    signal_real, signal_imag = forward(input_real, input_imag)
    kernel_real, kernel_imag = forward(filter_real, filter_imag)
    joint_real = signal_real * kernel_real - signal_imag * kernel_imag
    joint_imag = signal_real * kernel_imag + signal_imag * kernel_real
    back_cos, back_sin = tables(blocks, 2 * blocks, 2 * blocks)
    result_real = (product(back_cos, joint_real) - product(back_sin, joint_imag)) / (2 * blocks)
    result_imag = (product(back_cos, joint_imag) + product(back_sin, joint_real)) / (2 * blocks)
    return (result_real, result_imag)


def on_device(out_gate, key_proj, value_proj, long_filter, skip_gain, residual, norm_gain):
    chans, width = key_proj.shape
    blocks = lax.axis_size("seq")
    product_in = (key_proj.astype(jnp.float32) * value_proj.astype(jnp.float32)).astype(
        jnp.bfloat16
    )
    signal_f = product_in.astype(jnp.float32)
    whole_in, whole_filter = (
        lax.all_to_all(product_in, "seq", split_axis=0, concat_axis=1, tiled=True),
        lax.all_to_all(long_filter, "seq", split_axis=0, concat_axis=1, tiled=True),
    )
    group = whole_in.shape[0]

    def by_block(array):
        return (
            array.astype(jnp.float32)
            .reshape(group, blocks, width)
            .transpose(1, 0, 2)
            .reshape(blocks * group, width)
        )

    signal_real, signal_imag = block_spectrum(by_block(whole_in))
    kernel_real, kernel_imag = block_spectrum(by_block(whole_filter))
    result_real, result_imag = index_convolve(
        signal_real.reshape(blocks, -1),
        signal_imag.reshape(blocks, -1),
        kernel_real.reshape(blocks, -1),
        kernel_imag.reshape(blocks, -1),
    )
    timeline = block_inverse(
        result_real.reshape(blocks * group, 2 * width),
        result_imag.reshape(blocks * group, 2 * width),
    ).reshape(blocks, group, 2 * width)
    upper = timeline[:, :, width:]
    carried = jnp.concatenate([jnp.zeros((1, group, width), jnp.float32), upper[:-1]], axis=0)
    whole_out = (timeline[:, :, :width] + carried).transpose(1, 0, 2).reshape(group, blocks * width)
    convolved = lax.all_to_all(whole_out, "seq", split_axis=1, concat_axis=0, tiled=True)
    total = residual.astype(jnp.float32) + out_gate.astype(jnp.float32) * (
        convolved + skip_gain[:, None] * signal_f
    )
    squares = lax.psum(jnp.sum(total * total, axis=0), "ch")
    normed = total * lax.rsqrt(squares / D + 1e-06)[None, :] * norm_gain[:, None]
    return (total.astype(jnp.bfloat16), normed.astype(jnp.bfloat16))


def solution(mesh):
    return jax.shard_map(
        on_device,
        mesh=mesh,
        in_specs=(
            P("ch", "seq"),
            P("ch", "seq"),
            P("ch", "seq"),
            P("ch", "seq"),
            P("ch"),
            P("ch", "seq"),
            P("ch"),
        ),
        out_specs=(P("ch", "seq"), P("ch", "seq")),
        check_vma=False,
    )
```

profile of v0, /device:TPU:0, one launch (start us, length us, event | category | flops | bytes accessed | tf_op | source)
XLA Modules:
  0.0 86.7 jit_solution(10550059197464009538)
XLA Ops:
  0.6 1.1 %multiply_convert_fusion.1 = bf16[1024,128]{1,0:T(8,128)(2,1)S(1)} fusion(bf16[1024,128]{1,0:T(8,128)(2,1)} %param.9, bf16[1024,128]{1,0:T(8,128)(2,1)} %param.8), kind=kLoop, calls=%fused_computation.23 | loop fusion | flops 524288 | bytes 786432 | tf_op jit(solution)/shard_map/convert_element_type | solution.py:57
  1.7 11.9 %all_to_all.42 = bf16[8,128,128]{2,1,0:T(8,128)(2,1)S(1)} all-to-all(bf16[8,128,128]{2,1,0:T(8,128)(2,1)S(1)} %bitcast.44), channel_id=1, replica_groups=mesh['seq'=8,'ch'=4] {'seq'}, dimensions={0} | all-to-all | bytes 524288 | tf_op jit(solution)/shard_map/all_to_all | solution.py:62
  13.6 3.4 %all-to-all-start.1 = ((bf16[8,128,128]{2,1,0:T(8,128)(2,1)}), bf16[8,128,128]{2,1,0:T(8,128)(2,1)S(1)}, u32[]{:S(2)}, u32[]{:S(2)}) async-start(bf16[8,128,128]{2,1,0:T(8,128)(2,1)} %bitcast.45), calls=%async_computation.1 | async-start | bytes 524288 | tf_op jit(solution)/shard_map/all_to_all | solution.py:63
  17.1 1.1 %convolution_negate_fusion.1 = f32[1024,256]{1,0:T(8,128)S(1)} fusion(bf16[1024,128]{1,0:T(8,128)(2,1)S(1)} %bitcast.42), kind=kOutput, calls=%fused_computation.13 | convolution fusion | flops 403374080 | bytes 1310720 | tf_op jit(solution)/shard_map/dot_general | solution.py:19
  18.1 1.1 %fusion.27 = f32[1024,256]{1,0:T(8,128)S(1)} fusion(bf16[1024,128]{1,0:T(8,128)(2,1)S(1)} %bitcast.43), kind=kOutput, calls=%fused_computation.47 | convolution fusion | flops 403111936 | bytes 1310720 | tf_op jit(solution)/shard_map/dot_general | solution.py:19
  19.2 4.7 %all-to-all-done.1 = bf16[8,128,128]{2,1,0:T(8,128)(2,1)S(1)} async-done(((bf16[8,128,128]{2,1,0:T(8,128)(2,1)}), bf16[8,128,128]{2,1,0:T(8,128)(2,1)S(1)}, u32[]{:S(2)}, u32[]{:S(2)}) %all-to-all-start.1) | async-done | bytes 262176 | tf_op jit(solution)/shard_map/all_to_all | solution.py:63
  23.9 2.1 %fusion.2 = f32[1024,256]{0,1:T(8,128)} fusion(bf16[1024,128]{1,0:T(8,128)(2,1)S(1)} %bitcast.40), kind=kOutput, calls=%fused_computation.11 | convolution fusion | flops 403374080 | bytes 1310720 | tf_op jit(solution)/shard_map/dot_general | solution.py:19
  26.0 2.1 %convolution_bitcast_fusion = f32[1024,256]{0,1:T(8,128)} fusion(bf16[1024,128]{1,0:T(8,128)(2,1)S(1)} %bitcast.41), kind=kOutput, calls=%fused_computation.12 | convolution fusion | flops 403111936 | bytes 1310720 | tf_op jit(solution)/shard_map/dot_general | solution.py:19
  28.1 0.2 reshape.51
  28.3 1.2 %reshape.50 = f32[8,32768]{1,0:T(8,128)} reshape(f32[1024,256]{1,0:T(8,128)S(1)} %fusion.27) | data formatting | bytes 2097152 | tf_op jit(solution)/shard_map/reshape | solution.py:78
  29.4 0.0 copy-start.1
  29.4 2.6 %copy.10 = f32[1024,256]{1,0:T(8,128)} copy(f32[1024,256]{0,1:T(8,128)} %fusion.2) | data formatting | bytes 2097152 | tf_op jit(solution)/shard_map/neg | solution.py:25
  32.1 1.4 %reshape.54 = f32[8,32768]{1,0:T(8,128)S(1)} reshape(f32[1024,256]{1,0:T(8,128)} %copy.10) | data formatting | bytes 2097152 | tf_op jit(solution)/shard_map/reshape | solution.py:81
  33.5 0.0 copy-done.1
  33.5 1.4 %copy.9 = f32[1024,256]{1,0:T(8,128)} copy(f32[1024,256]{0,1:T(8,128)S(1)} %copy-done.1) | data formatting | bytes 2097152 | tf_op jit(solution)/shard_map/dot_general | solution.py:19
  34.8 1.4 %reshape.53 = f32[8,32768]{1,0:T(8,128)S(1)} reshape(f32[1024,256]{1,0:T(8,128)} %copy.9) | data formatting | bytes 2097152 | tf_op jit(solution)/shard_map/reshape | solution.py:80
  36.3 1.8 %fusion.46 = f32[16,32768]{1,0:T(8,128)S(1)} fusion(f32[8,32768]{1,0:T(8,128)S(1)} %reshape.53), kind=kOutput, calls=%fused_computation.67 | convolution fusion | flops 50333440 | bytes 3145728 | tf_op jit(solution)/shard_map/dot_general | solution.py:19
  38.1 1.8 %fusion.42 = f32[16,32768]{1,0:T(8,128)S(1)} fusion(f32[8,32768]{1,0:T(8,128)S(1)} %reshape.54), kind=kOutput, calls=%fused_computation.65 | convolution fusion | flops 50333440 | bytes 3145728 | tf_op jit(solution)/shard_map/dot_general | solution.py:19
  39.9 1.9 %convolution_add_fusion = f32[16,32768]{1,0:T(8,128)S(1)} fusion(f32[16,32768]{1,0:T(8,128)S(1)} %fusion.46, f32[8,32768]{1,0:T(8,128)S(1)} %reshape.54), kind=kOutput, calls=%fused_computation.2 | convolution fusion | flops 50857728 | bytes 5242880 | tf_op jit(solution)/shard_map/dot_general | solution.py:19
  41.8 0.0 copy-start
  41.8 2.1 %convolution_subtract_fusion = f32[16,32768]{1,0:T(8,128)S(1)} fusion(f32[16,32768]{1,0:T(8,128)S(1)} %fusion.42, f32[8,32768]{1,0:T(8,128)S(1)} %reshape.53), kind=kOutput, calls=%fused_computation | convolution fusion | flops 50857728 | bytes 5242880 | tf_op jit(solution)/shard_map/dot_general | solution.py:19
  43.9 0.0 copy-done
  43.9 1.8 %fusion.48 = f32[16,32768]{1,0:T(8,128)S(1)} fusion(f32[8,32768]{1,0:T(8,128)S(1)} %copy-done), kind=kOutput, calls=%fused_computation.68 | convolution fusion | flops 50333440 | bytes 3145728 | tf_op jit(solution)/shard_map/dot_general | solution.py:19
  45.8 1.8 %fusion.44 = f32[16,32768]{1,0:T(8,128)S(1)} fusion(f32[8,32768]{1,0:T(8,128)S(1)} %reshape.51), kind=kOutput, calls=%fused_computation.66 | convolution fusion | flops 50333440 | bytes 3145728 | tf_op jit(solution)/shard_map/dot_general | solution.py:19
  47.6 1.9 %convolution_add_fusion.1 = f32[16,32768]{1,0:T(8,128)S(1)} fusion(f32[16,32768]{1,0:T(8,128)S(1)} %fusion.48, f32[8,32768]{1,0:T(8,128)S(1)} %reshape.51), kind=kOutput, calls=%fused_computation.3 | convolution fusion | flops 50857728 | bytes 5242880 | tf_op jit(solution)/shard_map/dot_general | solution.py:19
  49.5 2.4 %multiply_add_fusion = (f32[16,32768]{1,0:T(8,128)S(1)}, f32[16,32768]{1,0:T(8,128)S(1)}) fusion(f32[16,32768]{1,0:T(8,128)S(1)} %convolution_add_fusion, f32[16,32768]{1,0:T(8,128)S(1)} %convolution_add_fusion.1, f32[16,32768]{1,0:T(8,128)S(1)} %convolution_subtract_fusion, f32[16,32768]{1,0:T(8,128)S(1)} %fusion.44, f32[8,32768]{1,0:T(8,128)S(1)} %copy-done), kind=kOutput, calls=%fused_computation.8 | convolution fusion | flops 54003456 | bytes 13631488 | tf_op jit(solution)/shard_map/dot_general | solution.py:19
  52.0 1.1 %fusion.59 = f32[8,32768]{1,0:T(8,128)S(1)} fusion(f32[16,32768]{1,0:T(8,128)S(1)} %get-tuple-element.4), kind=kOutput, calls=%fused_computation.74 | convolution fusion | flops 50333440 | bytes 3145728 | tf_op jit(solution)/shard_map/dot_general | solution.py:19
  53.1 1.1 %fusion.61 = f32[8,32768]{1,0:T(8,128)S(1)} fusion(f32[16,32768]{1,0:T(8,128)S(1)} %get-tuple-element.5), kind=kOutput, calls=%fused_computation.75 | convolution fusion | flops 50333440 | bytes 3145728 | tf_op jit(solution)/shard_map/dot_general | solution.py:19
  54.2 1.1 %fusion = f32[8,32768]{1,0:T(8,128)S(1)} fusion(f32[8,32768]{1,0:T(8,128)S(1)} %fusion.59, f32[16,32768]{1,0:T(8,128)S(1)} %get-tuple-element.5), kind=kOutput, calls=%fused_computation.5 | convolution fusion | flops 50857728 | bytes 4194304 | tf_op jit(solution)/shard_map/dot_general | solution.py:19
  55.4 1.1 %fusion.1 = f32[8,32768]{1,0:T(8,128)S(1)} fusion(f32[8,32768]{1,0:T(8,128)S(1)} %fusion.61, f32[16,32768]{1,0:T(8,128)S(1)} %get-tuple-element.4), kind=kOutput, calls=%fused_computation.7 | convolution fusion | flops 50857728 | bytes 4194304 | tf_op jit(solution)/shard_map/dot_general | solution.py:19
  56.5 0.2 reshape.55
  56.7 2.2 %fusion.11 = f32[1024,256]{1,0:T(8,128)S(1)} fusion(f32[1024,256]{1,0:T(8,128)S(1)} %reshape.55), kind=kOutput, calls=%fused_computation.31 | convolution fusion | flops 806223872 | bytes 2097152 | tf_op jit(solution)/shard_map/dot_general | solution.py:19
  58.9 0.2 reshape.56
  59.1 2.0 %fusion.3 = f32[1024,256]{1,0:T(8,128)S(1)} fusion(f32[1024,256]{1,0:T(8,128)S(1)} %fusion.11, f32[1024,256]{1,0:T(8,128)S(1)} %reshape.56), kind=kOutput, calls=%fused_computation.15 | convolution fusion | flops 806748160 | bytes 3145728 | tf_op jit(solution)/shard_map/dot_general | solution.py:19
  61.0 0.0 copy-start.2
  61.1 0.0 copy-start.3
  61.1 0.0 copy-start.4
  61.1 0.0 copy-start.5
  61.1 0.1 fusion.4
  61.2 12.3 %all_to_all.43 = f32[128,8,128]{2,0,1:T(8,128)S(1)} all-to-all(f32[128,8,128]{2,0,1:T(8,128)S(1)} %fusion.4), channel_id=1, replica_groups=mesh['seq'=8,'ch'=4] {'seq'}, dimensions={1} | all-to-all | bytes 1048576 | tf_op jit(solution)/shard_map/all_to_all | solution.py:90
  73.5 0.0 copy-done.2
  73.5 0.0 copy-done.3
  73.5 0.0 copy-done.4
  73.5 0.3 multiply_reduce_fusion
  73.7 12.0 %psum.7 = f32[128]{0:T(128)S(1)} all-reduce(f32[128]{0:T(128)S(1)} %get-tuple-element.2), channel_id=1, replica_groups=mesh['seq'=8,'ch'=4] {'ch'}, use_global_device_ids=true, to_apply=%region_1.2 | all-reduce | flops 128 | bytes 1024 | tf_op jit(solution)/shard_map/psum | solution.py:94
  85.7 0.0 copy-done.5
  85.7 1.0 %multiply_convert_fusion = (bf16[1024,128]{1,0:T(8,128)(2,1)}, bf16[1024,128]{1,0:T(8,128)(2,1)}) fusion(f32[1024,128]{1,0:T(8,128)S(1)} %get-tuple-element.3, f32[1024]{0:T(1024)S(1)} %copy-done.5, f32[128]{0:T(128)S(1)} %add_rsqrt_fusion), kind=kLoop, calls=%fused_computation.21 | loop fusion | flops 524288 | bytes 1053184 | tf_op jit(solution)/shard_map/convert_element_type | solution.py:96
  (2 shorter events, 0.0 us)
Async XLA Ops:
  13.6 10.3 %all-to-all-start.1 = ((bf16[8,128,128]{2,1,0:T(8,128)(2,1)}), bf16[8,128,128]{2,1,0:T(8,128)(2,1)S(1)}, u32[]{:S(2)}, u32[]{:S(2)}) async-start(bf16[8,128,128]{2,1,0:T(8,128)(2,1)} %bitcast.45), calls=%async_computation.1 | async-start | bytes 524288 | tf_op jit(solution)/shard_map/all_to_all | solution.py:63
  29.4 4.0 %copy-start.1 = (f32[1024,256]{0,1:T(8,128)S(1)}, f32[1024,256]{0,1:T(8,128)}, u32[]{:S(2)}) copy-start(f32[1024,256]{0,1:T(8,128)} %convolution_bitcast_fusion) | copy-start | bytes 3145732
  41.8 2.1 %copy-start = (f32[8,32768]{1,0:T(8,128)S(1)}, f32[8,32768]{1,0:T(8,128)}, u32[]{:S(2)}) copy-start(f32[8,32768]{1,0:T(8,128)} %reshape.50) | copy-start | bytes 3145732
  61.0 12.4 %copy-start.2 = (bf16[1024,128]{1,0:T(8,128)(2,1)S(1)}, bf16[1024,128]{1,0:T(8,128)(2,1)}, u32[]{:S(2)}) copy-start(bf16[1024,128]{1,0:T(8,128)(2,1)} %param.7) | copy-start | bytes 786436
  61.1 12.4 %copy-start.3 = (bf16[1024,128]{1,0:T(8,128)(2,1)S(1)}, bf16[1024,128]{1,0:T(8,128)(2,1)}, u32[]{:S(2)}) copy-start(bf16[1024,128]{1,0:T(8,128)(2,1)} %param.12) | copy-start | bytes 786436
  61.1 12.4 %copy-start.4 = (f32[1024]{0:T(1024)S(1)}, f32[1024]{0:T(1024)}, u32[]{:S(2)}) copy-start(f32[1024]{0:T(1024)} %param.11) | copy-start | bytes 12292
  61.1 24.6 %copy-start.5 = (f32[1024]{0:T(1024)S(1)}, f32[1024]{0:T(1024)}, u32[]{:S(2)}) copy-start(f32[1024]{0:T(1024)} %param.13) | copy-start | bytes 12292
where the time goes:
time: 87.1 us; the launch traced here: 86.7 us
  blocking collectives  36.1 us (41%)
  matrix products  30.6 us (35%)
  local copies, waits for them, and re-layouts  8.56 us (10%)
  waiting for transfers between devices  4.67 us (5%)
  starting transfers between devices  3.41 us (4%)
  other arithmetic  2.43 us (3%)
    dot_general x18, matrix products, product(): jnp.dot(left, right, precision=HIGHEST, preferred_element_type=jnp.float32)  30.6 us
    all_to_all x1, blocking collectives, on_device(): lax.all_to_all(whole_out, 'seq', split_axis=1, concat_axis=0, tiled=True)  12.3 us
    psum x1, blocking collectives, on_device(): squares = lax.psum(jnp.sum(total * total, axis=0), 'ch')  12 us
    all_to_all x1, blocking collectives, on_device(): lax.all_to_all(product_in, 'seq', split_axis=0, concat_axis=1, tiled=True)  11.9 us
    all_to_all x1, waiting for transfers between devices, on_device(): lax.all_to_all(long_filter, 'seq', split_axis=0, concat_axis=1, tiled=True)  4.67 us
    all_to_all x1, starting transfers between devices, on_device(): lax.all_to_all(long_filter, 'seq', split_axis=0, concat_axis=1, tiled=True)  3.41 us
    neg x1, local copies, waits for them, and re-layouts, block_spectrum(): return (product(signal, cosine), -product(signal, sine))  2.63 us
  transfers between devices with their start and end apart: 1, of which 1 were waited for; matrix products, arithmetic and copies ran while one was open for 2% of the time, Pallas kernels for 0%

commit v1 on v0

--- a/solution.py
+++ b/solution.py
@@ -60,7 +60,12 @@
     signal_f = product_in.astype(jnp.float32)
     whole_in, whole_filter = (
         lax.all_to_all(product_in, "seq", split_axis=0, concat_axis=1, tiled=True),
-        lax.all_to_all(long_filter, "seq", split_axis=0, concat_axis=1, tiled=True),
+        jnp.concatenate(
+            lax.all_to_all(
+                jnp.stack(jnp.split(long_filter, lax.axis_size("seq"), axis=0)), "seq", 0, 0
+            ),
+            axis=1,
+        ),
     )
     group = whole_in.shape[0]
 

time: 87.1 us -> 101 us (1.16); the launches traced: 86.7 us -> 99.4 us
  blocking collectives: 36.1 us -> 24.2 us
  matrix products: 30.6 us -> 40.1 us
  local copies, waits for them, and re-layouts: 8.56 us -> 16.1 us
  starting transfers between devices: 3.41 us -> 9.4 us
  other arithmetic: 2.43 us -> 4.1 us
    all_to_all x1 -> x0, blocking collectives: 11.9 us -> none  [on_device(): lax.all_to_all(product_in, 'seq', split_axis=0, concat_axis=1, tiled=True)]
    unnamed x12 -> x25, local copies, waits for them, and re-layouts: 0.03 us -> 9.94 us
    dot_general x18, matrix products: 30.6 us -> 40.1 us  [product(): jnp.dot(left, right, precision=HIGHEST, preferred_element_type=jnp.float32)]
    all_to_all x1 -> x2, starting transfers between devices: 3.41 us -> 9.4 us  [the longest x1 5.2 us: on_device(): lax.all_to_all(product_in, 'seq', split_axis=0, concat_axis=1, tiled=True)]
    neg x1 -> x0, local copies, waits for them, and re-layouts: 2.63 us -> none  [block_spectrum(): return (product(signal, cosine), -product(signal, sine))]
    another operation x0 -> x1, local copies, waits for them, and re-layouts: none -> 1.37 us  [on_device(): jnp.stack(jnp.split(long_filter, lax.axis_size('seq'), axis=0))]
    dot_general x1 -> x0, local copies, waits for them, and re-layouts: 1.36 us -> none  [product(): jnp.dot(left, right, precision=HIGHEST, preferred_element_type=jnp.float32)]
    reshape x1, local copies, waits for them, and re-layouts: 1.42 us -> 0.19 us  [on_device(): kernel_imag.reshape(blocks, -1)]
  transfers between devices with their start and end apart: 1 -> 2, of which waited for: 1 -> 1; matrix products, arithmetic and copies ran while one was open for 2% -> 13% of each run, Pallas kernels for 0% -> 0%
where the time goes in v1:
time: 101 us; the launch traced here: 99.4 us
  matrix products  40.1 us (40%)
  blocking collectives  24.2 us (24%)
  local copies, waits for them, and re-layouts  16.1 us (16%)
  starting transfers between devices  9.4 us (9%)
  waiting for transfers between devices  4.74 us (5%)
  other arithmetic  4.1 us (4%)
    dot_general x18, matrix products, product(): jnp.dot(left, right, precision=HIGHEST, preferred_element_type=jnp.float32)  40.1 us
    all_to_all x1, blocking collectives, on_device(): lax.all_to_all(whole_out, 'seq', split_axis=1, concat_axis=0, tiled=True)  12.3 us
    psum x1, blocking collectives, on_device(): squares = lax.psum(jnp.sum(total * total, axis=0), 'ch')  12 us
    unnamed x25, local copies, waits for them, and re-layouts  9.94 us
    all_to_all x1, starting transfers between devices, on_device(): lax.all_to_all(product_in, 'seq', split_axis=0, concat_axis=1, tiled=True)  5.2 us
    all_to_all x1, waiting for transfers between devices, on_device(): lax.all_to_all(jnp.stack(jnp.split(long_filter, lax.axis_size('seq'), axi...  4.74 us
    all_to_all x1, starting transfers between devices, on_device(): lax.all_to_all(jnp.stack(jnp.split(long_filter, lax.axis_size('seq'), axi...  4.2 us
  transfers between devices with their start and end apart: 2, of which 1 were waited for; matrix products, arithmetic and copies ran while one was open for 13% of the time, Pallas kernels for 0%

profile of v1, /device:TPU:0, one launch (start us, length us, event | category | flops | bytes accessed | tf_op | source)
XLA Modules:
  0.0 99.4 jit_solution(5487335403993297737)
XLA Ops:
  0.6 1.8 %multiply_convert_fusion.1 = bf16[1024,128]{1,0:T(8,128)(2,1)} fusion(bf16[1024,128]{1,0:T(8,128)(2,1)} %param.9, bf16[1024,128]{1,0:T(8,128)(2,1)} %param.8), kind=kLoop, calls=%fused_computation.21 | loop fusion | flops 524288 | bytes 786432 | tf_op jit(solution)/shard_map/convert_element_type | solution.py:57
  2.4 5.2 %all-to-all-start = ((bf16[8,128,128]{2,1,0:T(8,128)(2,1)}), bf16[8,128,128]{2,1,0:T(8,128)(2,1)S(1)}, u32[]{:S(2)}, u32[]{:S(2)}) async-start(bf16[8,128,128]{2,1,0:T(8,128)(2,1)} %bitcast), calls=%async_computation | async-start | bytes 524288 | tf_op jit(solution)/shard_map/all_to_all | solution.py:62
  7.6 1.4 %bitcast_dynamic-update-slice_fusion.7 = bf16[8,128,128]{2,1,0:T(8,128)(2,1)} fusion(bf16[1024,128]{1,0:T(8,128)(2,1)} %param.10), kind=kLoop, calls=%fused_computation.54 | loop fusion | bytes 65536
  9.0 1.4 %bitcast_dynamic-update-slice_fusion.6 = bf16[8,128,128]{2,1,0:T(8,128)(2,1)} fusion(bf16[8,128,128]{2,1,0:T(8,128)(2,1)} %bitcast_dynamic-update-slice_fusion.7, bf16[1024,128]{1,0:T(8,128)(2,1)} %param.10), kind=kLoop, calls=%fused_computation.53 | loop fusion | bytes 65536
  10.4 1.4 %bitcast_dynamic-update-slice_fusion.5 = bf16[8,128,128]{2,1,0:T(8,128)(2,1)} fusion(bf16[8,128,128]{2,1,0:T(8,128)(2,1)} %bitcast_dynamic-update-slice_fusion.6, bf16[1024,128]{1,0:T(8,128)(2,1)} %param.10), kind=kLoop, calls=%fused_computation.52 | loop fusion | bytes 65536
  11.8 1.4 %bitcast_dynamic-update-slice_fusion.4 = bf16[8,128,128]{2,1,0:T(8,128)(2,1)} fusion(bf16[8,128,128]{2,1,0:T(8,128)(2,1)} %bitcast_dynamic-update-slice_fusion.5, bf16[1024,128]{1,0:T(8,128)(2,1)} %param.10), kind=kLoop, calls=%fused_computation.51 | loop fusion | bytes 65536
  13.1 1.4 %bitcast_dynamic-update-slice_fusion.3 = bf16[8,128,128]{2,1,0:T(8,128)(2,1)} fusion(bf16[8,128,128]{2,1,0:T(8,128)(2,1)} %bitcast_dynamic-update-slice_fusion.4, bf16[1024,128]{1,0:T(8,128)(2,1)} %param.10), kind=kLoop, calls=%fused_computation.50 | loop fusion | bytes 65536
  14.5 1.4 %bitcast_dynamic-update-slice_fusion.2 = bf16[8,128,128]{2,1,0:T(8,128)(2,1)} fusion(bf16[8,128,128]{2,1,0:T(8,128)(2,1)} %bitcast_dynamic-update-slice_fusion.3, bf16[1024,128]{1,0:T(8,128)(2,1)} %param.10), kind=kLoop, calls=%fused_computation.49 | loop fusion | bytes 65536
  15.9 1.4 %bitcast_dynamic-update-slice_fusion.1 = bf16[8,128,128]{2,1,0:T(8,128)(2,1)} fusion(bf16[8,128,128]{2,1,0:T(8,128)(2,1)} %bitcast_dynamic-update-slice_fusion.2, bf16[1024,128]{1,0:T(8,128)(2,1)} %param.10), kind=kLoop, calls=%fused_computation.48 | loop fusion | bytes 65536
  17.3 1.4 %bitcast_dynamic-update-slice_fusion = bf16[8,128,128]{2,1,0:T(8,128)(2,1)} fusion(bf16[8,128,128]{2,1,0:T(8,128)(2,1)} %bitcast_dynamic-update-slice_fusion.1, bf16[1024,128]{1,0:T(8,128)(2,1)} %param.10), kind=kLoop, calls=%fused_computation.47 | loop fusion | bytes 65536 | tf_op jit(solution)/shard_map/stack | solution.py:65
  18.6 0.0 all-to-all-done
  18.6 4.2 %all-to-all-start.1 = ((bf16[8,128,128]{2,1,0:T(8,128)(2,1)}), bf16[8,128,128]{2,1,0:T(8,128)(2,1)S(1)}, u32[]{:S(2)}, u32[]{:S(2)}) async-start(bf16[8,128,128]{2,1,0:T(8,128)(2,1)} %bitcast_dynamic-update-slice_fusion), calls=%async_computation.1 | async-start | bytes 524288 | tf_op jit(solution)/shard_map/all_to_all | solution.py:64
  22.8 1.1 %fusion.27 = f32[1024,256]{1,0:T(8,128)S(1)} fusion(bf16[1024,128]{1,0:T(8,128)(2,1)S(1)} %bitcast.51), kind=kOutput, calls=%fused_computation.46 | convolution fusion | flops 403111936 | bytes 1310720 | tf_op jit(solution)/shard_map/dot_general | solution.py:19
  23.9 1.1 %convolution_negate_fusion.1 = f32[1024,256]{1,0:T(8,128)S(1)} fusion(bf16[1024,128]{1,0:T(8,128)(2,1)S(1)} %bitcast.52), kind=kOutput, calls=%fused_computation.11 | convolution fusion | flops 403374080 | bytes 1310720 | tf_op jit(solution)/shard_map/dot_general | solution.py:19
  25.0 4.7 %all-to-all-done.1 = bf16[8,128,128]{2,1,0:T(8,128)(2,1)S(1)} async-done(((bf16[8,128,128]{2,1,0:T(8,128)(2,1)}), bf16[8,128,128]{2,1,0:T(8,128)(2,1)S(1)}, u32[]{:S(2)}, u32[]{:S(2)}) %all-to-all-start.1) | async-done | bytes 262176 | tf_op jit(solution)/shard_map/all_to_all | solution.py:64
  29.7 2.0 %convolution_negate_fusion = f32[1024,256]{1,0:T(8,128)} fusion(bf16[1024,128]{1,0:T(8,128)(2,1)S(1)} %bitcast.53), kind=kOutput, calls=%fused_computation.10 | convolution fusion | flops 403374080 | bytes 1310720 | tf_op jit(solution)/shard_map/dot_general | solution.py:19
  31.8 2.1 %fusion.25 = f32[1024,256]{1,0:T(8,128)} fusion(bf16[1024,128]{1,0:T(8,128)(2,1)S(1)} %bitcast.54), kind=kOutput, calls=%fused_computation.45 | convolution fusion | flops 403111936 | bytes 1310720 | tf_op jit(solution)/shard_map/dot_general | solution.py:19
  33.9 0.2 reshape.49
  34.0 3.1 %fusion.48 = f32[16,32768]{1,0:T(8,128)} fusion(f32[8,32768]{1,0:T(8,128)S(1)} %reshape.49), kind=kOutput, calls=%fused_computation.75 | convolution fusion | flops 50333440 | bytes 3145728 | tf_op jit(solution)/shard_map/dot_general | solution.py:19
  37.2 0.2 reshape.50
  37.4 3.2 %fusion.44 = f32[16,32768]{1,0:T(8,128)} fusion(f32[8,32768]{1,0:T(8,128)S(1)} %reshape.50), kind=kOutput, calls=%fused_computation.73 | convolution fusion | flops 50333440 | bytes 3145728 | tf_op jit(solution)/shard_map/dot_general | solution.py:19
  40.6 3.2 %convolution_add_fusion.1 = f32[16,32768]{1,0:T(8,128)} fusion(f32[16,32768]{1,0:T(8,128)S(1)} %copy-done, f32[8,32768]{1,0:T(8,128)S(1)} %reshape.50), kind=kOutput, calls=%fused_computation.3 | convolution fusion | flops 50857728 | bytes 5242880 | tf_op jit(solution)/shard_map/dot_general | solution.py:19
  43.7 0.2 reshape.53
  43.9 3.2 %fusion.42 = f32[16,32768]{1,0:T(8,128)} fusion(f32[8,32768]{1,0:T(8,128)S(1)} %reshape.53), kind=kOutput, calls=%fused_computation.72 | convolution fusion | flops 50333440 | bytes 3145728 | tf_op jit(solution)/shard_map/dot_general | solution.py:19
  47.1 1.4 %reshape.52 = f32[8,32768]{1,0:T(8,128)S(1)} reshape(f32[1024,256]{1,0:T(8,128)} %fusion.25) | data formatting | bytes 2097152 | tf_op jit(solution)/shard_map/reshape | solution.py:85
  48.5 2.0 %fusion.46 = f32[16,32768]{1,0:T(8,128)S(1)} fusion(f32[8,32768]{1,0:T(8,128)S(1)} %reshape.52), kind=kOutput, calls=%fused_computation.74 | convolution fusion | flops 50333440 | bytes 3145728 | tf_op jit(solution)/shard_map/dot_general | solution.py:19
  50.5 1.9 %convolution_subtract_fusion = f32[16,32768]{1,0:T(8,128)S(1)} fusion(f32[16,32768]{1,0:T(8,128)S(1)} %copy-done.1, f32[8,32768]{1,0:T(8,128)S(1)} %reshape.52), kind=kOutput, calls=%fused_computation | convolution fusion | flops 50857728 | bytes 5242880 | tf_op jit(solution)/shard_map/dot_general | solution.py:19
  52.5 1.9 %convolution_add_fusion = f32[16,32768]{1,0:T(8,128)S(1)} fusion(f32[16,32768]{1,0:T(8,128)S(1)} %fusion.46, f32[8,32768]{1,0:T(8,128)S(1)} %reshape.53), kind=kOutput, calls=%fused_computation.2 | convolution fusion | flops 50857728 | bytes 5242880 | tf_op jit(solution)/shard_map/dot_general | solution.py:19
  54.4 0.3 copy-done.3
  54.7 2.5 %multiply_add_fusion = (f32[16,32768]{1,0:T(8,128)S(1)}, f32[16,32768]{1,0:T(8,128)S(1)}) fusion(f32[16,32768]{1,0:T(8,128)S(1)} %convolution_add_fusion, f32[16,32768]{1,0:T(8,128)S(1)} %copy-done.3, f32[16,32768]{1,0:T(8,128)S(1)} %convolution_subtract_fusion, f32[16,32768]{1,0:T(8,128)S(1)} %copy-done.2, f32[8,32768]{1,0:T(8,128)S(1)} %reshape.49), kind=kOutput, calls=%fused_computation.8 | convolution fusion | flops 54003456 | bytes 13631488 | tf_op jit(solution)/shard_map/dot_general | solution.py:19
  57.1 1.1 %fusion.59 = f32[8,32768]{1,0:T(8,128)S(1)} fusion(f32[16,32768]{1,0:T(8,128)S(1)} %get-tuple-element.4), kind=kOutput, calls=%fused_computation.81 | convolution fusion | flops 50333440 | bytes 3145728 | tf_op jit(solution)/shard_map/dot_general | solution.py:19
  58.3 2.1 %fusion.61 = f32[8,32768]{1,0:T(8,128)} fusion(f32[16,32768]{1,0:T(8,128)S(1)} %get-tuple-element.5), kind=kOutput, calls=%fused_computation.82 | convolution fusion | flops 50333440 | bytes 3145728 | tf_op jit(solution)/shard_map/dot_general | solution.py:19
  60.4 2.2 %fusion = f32[8,32768]{1,0:T(8,128)} fusion(f32[8,32768]{1,0:T(8,128)S(1)} %fusion.59, f32[16,32768]{1,0:T(8,128)S(1)} %get-tuple-element.5), kind=kOutput, calls=%fused_computation.5 | convolution fusion | flops 50857728 | bytes 4194304 | tf_op jit(solution)/shard_map/dot_general | solution.py:19
  62.5 1.4 %reshape.55 = f32[1024,256]{1,0:T(8,128)S(1)} reshape(f32[8,32768]{1,0:T(8,128)} %fusion) | data formatting | bytes 2097152 | tf_op jit(solution)/shard_map/reshape | solution.py:90
  63.9 3.3 %fusion.1 = f32[8,32768]{1,0:T(8,128)} fusion(f32[8,32768]{1,0:T(8,128)} %fusion.61, f32[16,32768]{1,0:T(8,128)S(1)} %get-tuple-element.4), kind=kOutput, calls=%fused_computation.7 | convolution fusion | flops 50857728 | bytes 4194304 | tf_op jit(solution)/shard_map/dot_general | solution.py:19
  67.3 1.4 %reshape.54 = f32[1024,256]{1,0:T(8,128)S(1)} reshape(f32[8,32768]{1,0:T(8,128)} %fusion.1) | data formatting | bytes 2097152 | tf_op jit(solution)/shard_map/reshape | solution.py:89
  68.7 2.2 %fusion.10 = f32[1024,256]{1,0:T(8,128)S(1)} fusion(f32[1024,256]{1,0:T(8,128)S(1)} %reshape.54), kind=kOutput, calls=%fused_computation.29 | convolution fusion | flops 806223872 | bytes 2097152 | tf_op jit(solution)/shard_map/dot_general | solution.py:19
  70.8 2.0 %fusion.2 = f32[1024,256]{1,0:T(8,128)S(1)} fusion(f32[1024,256]{1,0:T(8,128)S(1)} %fusion.10, f32[1024,256]{1,0:T(8,128)S(1)} %reshape.55), kind=kOutput, calls=%fused_computation.13 | convolution fusion | flops 806748160 | bytes 3145728 | tf_op jit(solution)/shard_map/dot_general | solution.py:19
  72.8 0.0 copy-start.5
  72.8 0.0 copy-start.6
  72.8 0.0 copy-start.7
  72.9 0.0 copy-start.8
  72.9 0.1 fusion.3
  73.0 12.3 %all_to_all.34 = f32[128,8,128]{2,0,1:T(8,128)S(1)} all-to-all(f32[128,8,128]{2,0,1:T(8,128)S(1)} %fusion.3), channel_id=1, replica_groups=mesh['seq'=8,'ch'=4] {'seq'}, dimensions={1} | all-to-all | bytes 1048576 | tf_op jit(solution)/shard_map/all_to_all | solution.py:95
  85.3 1.2 %multiply_reduce_fusion = (f32[128]{0:T(128)S(1)}, f32[1024,128]{1,0:T(8,128)S(1)}) fusion(bf16[1024,128]{1,0:T(8,128)(2,1)} %multiply_convert_fusion.1, f32[1024]{0:T(1024)S(1)} %copy-done.7, f32[128,8,128]{2,0,1:T(8,128)S(1)} %all_to_all.34, bf16[1024,128]{1,0:T(8,128)(2,1)S(1)} %copy-done.5, bf16[1024,128]{1,0:T(8,128)(2,1)S(1)} %copy-done.6), kind=kLoop, calls=%fused_computation.20 | loop fusion | flops 1179520 | bytes 1839616 | tf_op jit(solution)/shard_map/reduce_sum | solution.py:99
  86.5 12.0 %psum.7 = f32[128]{0:T(128)S(1)} all-reduce(f32[128]{0:T(128)S(1)} %get-tuple-element.2), channel_id=1, replica_groups=mesh['seq'=8,'ch'=4] {'ch'}, use_global_device_ids=true, to_apply=%region_1.2 | all-reduce | flops 128 | bytes 1024 | tf_op jit(solution)/shard_map/psum | solution.py:99
  98.5 0.0 copy-done.8
  98.5 1.0 multiply_convert_fusion
  (14 shorter events, 0.1 us)
Async XLA Ops:
  2.4 16.2 %all-to-all-start = ((bf16[8,128,128]{2,1,0:T(8,128)(2,1)}), bf16[8,128,128]{2,1,0:T(8,128)(2,1)S(1)}, u32[]{:S(2)}, u32[]{:S(2)}) async-start(bf16[8,128,128]{2,1,0:T(8,128)(2,1)} %bitcast), calls=%async_computation | async-start | bytes 524288 | tf_op jit(solution)/shard_map/all_to_all | solution.py:62
  18.6 11.1 %all-to-all-start.1 = ((bf16[8,128,128]{2,1,0:T(8,128)(2,1)}), bf16[8,128,128]{2,1,0:T(8,128)(2,1)S(1)}, u32[]{:S(2)}, u32[]{:S(2)}) async-start(bf16[8,128,128]{2,1,0:T(8,128)(2,1)} %bitcast_dynamic-update-slice_fusion), calls=%async_computation.1 | async-start | bytes 524288 | tf_op jit(solution)/shard_map/all_to_all | solution.py:64
  37.4 3.2 %copy-start = (f32[16,32768]{1,0:T(8,128)S(1)}, f32[16,32768]{1,0:T(8,128)}, u32[]{:S(2)}) copy-start(f32[16,32768]{1,0:T(8,128)} %fusion.48) | copy-start | bytes 6291460
  40.6 3.2 %copy-start.4 = (f32[1024,256]{1,0:T(8,128)S(1)}, f32[1024,256]{1,0:T(8,128)}, u32[]{:S(2)}) copy-start(f32[1024,256]{1,0:T(8,128)} %convolution_negate_fusion) | copy-start | bytes 3145732
  48.5 2.0 %copy-start.1 = (f32[16,32768]{1,0:T(8,128)S(1)}, f32[16,32768]{1,0:T(8,128)}, u32[]{:S(2)}) copy-start(f32[16,32768]{1,0:T(8,128)} %fusion.42) | copy-start | bytes 6291460
  52.4 1.9 %copy-start.2 = (f32[16,32768]{1,0:T(8,128)S(1)}, f32[16,32768]{1,0:T(8,128)}, u32[]{:S(2)}) copy-start(f32[16,32768]{1,0:T(8,128)} %fusion.44) | copy-start | bytes 6291460
  52.5 2.2 %copy-start.3 = (f32[16,32768]{1,0:T(8,128)S(1)}, f32[16,32768]{1,0:T(8,128)}, u32[]{:S(2)}) copy-start(f32[16,32768]{1,0:T(8,128)} %convolution_add_fusion.1) | copy-start | bytes 6291460
  72.8 12.4 %copy-start.5 = (bf16[1024,128]{1,0:T(8,128)(2,1)S(1)}, bf16[1024,128]{1,0:T(8,128)(2,1)}, u32[]{:S(2)}) copy-start(bf16[1024,128]{1,0:T(8,128)(2,1)} %param.7) | copy-start | bytes 786436
  72.8 12.4 %copy-start.6 = (bf16[1024,128]{1,0:T(8,128)(2,1)S(1)}, bf16[1024,128]{1,0:T(8,128)(2,1)}, u32[]{:S(2)}) copy-start(bf16[1024,128]{1,0:T(8,128)(2,1)} %param.12) | copy-start | bytes 786436
  72.8 12.4 %copy-start.7 = (f32[1024]{0:T(1024)S(1)}, f32[1024]{0:T(1024)}, u32[]{:S(2)}) copy-start(f32[1024]{0:T(1024)} %param.11) | copy-start | bytes 12292
  72.9 25.6 %copy-start.8 = (f32[1024]{0:T(1024)S(1)}, f32[1024]{0:T(1024)}, u32[]{:S(2)}) copy-start(f32[1024]{0:T(1024)} %param.13) | copy-start | bytes 12292
